TPU v7x, 512 devices: a whole 4x4x16 slice. The times are simulated.
512 devices in a mesh: exp: 64 (over x, z), rep: 8 (over y, core).
Axes of the slice: x: 4, y: 4, z: 16, core: 2. Of those that a mesh axis runs over, the one named last changes fastest.
Arguments:
- latent: bfloat16 [128, 16, 64], P('exp'), may hold values from -6 to 6
- stem_weight: bfloat16 [144, 1536], replicated, may hold values from -0.5 to 0.5
- norm_gain: float32 [1536], replicated, may hold values from 0.4 to 1.6
- router_weight: bfloat16 [1536, 8], replicated, may hold values from -0.15625 to 0.15625
- routes: int32 [8192, 2], P('exp'), may hold values from 0 to 7, all different within a row; in each aligned block of 128 rows (0 to 127, 128 to 255, ...) at most 40 rows name the same one
- gate_weight: bfloat16 [1536, 24576], P('rep', 'exp'), may hold values from -0.15625 to 0.15625
- up_weight: bfloat16 [1536, 24576], P('rep', 'exp'), may hold values from -0.15625 to 0.15625
- down_weight: bfloat16 [24576, 1536], P('exp', 'rep'), may hold values from -0.109375 to 0.109375
- grad_mixed: bfloat16 [8192, 1536], P('exp'), may hold values from -6 to 6
Outputs:
- mixed: bfloat16 [8192, 1536], P('exp')
- grad_latent: float32 [128, 16, 64], P('exp')
- grad_gate: float32 [1536, 24576], P('rep', 'exp')
- grad_up: float32 [1536, 24576], P('rep', 'exp')
- grad_down: float32 [24576, 1536], P('exp', 'rep')
Inputs may be any that keep to these rules, and one draw needn't show every extreme that they name: `routes`: A token's 2 experts differ. Within the 128 tokens of one device, no expert is named more than 40 times, and in every draw some device's tokens name some expert exactly 40 times.
All inputs are finite; a program needn't handle non-finite values.
Results may differ from a plain program's by a relative error of at most 0.023.
Values may be sent and summed in bfloat16 or wider, within the bound.
A program may use at most 64 MiB of HBM per device.

v0:
```python
import jax
import jax.numpy as jnp
from jax import lax
from jax.sharding import PartitionSpec as P

CAP = 40


def with_halo(cells, sides, width):
    for axis, dim in sides:
        count = lax.axis_size(axis)
        ends = count - 1
        head = lax.slice_in_dim(cells, 0, width, axis=dim)
        tail = lax.slice_in_dim(cells, cells.shape[dim] - width, cells.shape[dim], axis=dim)
        cells = jnp.concatenate(
            [
                lax.ppermute(tail, axis, [(i, (i + 1) % count) for i in range(ends)]),
                cells,
                lax.ppermute(head, axis, [((i + 1) % count, i) for i in range(ends)]),
            ],
            axis=dim,
        )
    return cells


def rms_norm(values, gain):
    return values * lax.rsqrt(jnp.mean(values * values, axis=-1, keepdims=True) + 1e-06) * gain


def gating(picked):
    chosen = jax.nn.sigmoid(picked)
    return chosen / jnp.sum(chosen, axis=-1, keepdims=True)


def local(
    latent,
    stem_weight,
    norm_gain,
    router_weight,
    routes,
    gate_weight,
    up_weight,
    down_weight,
    grad_mixed,
):
    rows_here = latent.shape[0]
    channels = latent.shape[1]
    width = latent.shape[2]
    model_width = stem_weight.shape[1]
    experts = router_weight.shape[1]
    top_count = routes.shape[1]
    tok_here = rows_here * width
    shards = lax.axis_size("exp") // experts
    group_size = CAP // lax.axis_size("rep")
    slots = experts * CAP
    padded = with_halo(latent, (("exp", 0),), 1)
    padded = jnp.pad(padded, ((0, 0), (0, 0), (1, 1)))
    pieces = jnp.stack(
        [padded[i : i + rows_here, :, j : j + width] for i in range(3) for j in range(3)], axis=0
    )
    patches = jnp.transpose(pieces, (1, 3, 0, 2)).reshape(tok_here, 9 * channels)
    stem = jnp.dot(patches, stem_weight, preferred_element_type=jnp.float32).astype(jnp.bfloat16)
    stem_value = stem.astype(jnp.float32)
    normed = rms_norm(stem_value, norm_gain).astype(jnp.bfloat16)
    logits = jnp.dot(normed, router_weight, preferred_element_type=jnp.float32)
    picked = jnp.take_along_axis(logits, routes, axis=1)
    gates = gating(picked)
    upstream = grad_mixed.astype(jnp.float32)
    grad_rows = (
        (gates[:, :, None] * upstream[:, None, :]).astype(jnp.bfloat16).reshape(-1, model_width)
    )
    flat_routes = routes.reshape(-1)
    onehot = (flat_routes[:, None] == jnp.arange(experts, dtype=jnp.int32)[None, :]).astype(
        jnp.int32
    )
    position = jnp.sum(onehot * (jnp.cumsum(onehot, axis=0) - 1), axis=1)
    slot_index = flat_routes * CAP + position
    send_rows = (
        jnp.zeros((slots, model_width), jnp.bfloat16)
        .at[slot_index]
        .set(jnp.repeat(normed, top_count, axis=0))
    )
    send_grads = jnp.zeros((slots, model_width), jnp.bfloat16).at[slot_index].set(grad_rows)
    group_start = lax.axis_index("rep") * group_size
    group_rows = lax.dynamic_slice_in_dim(
        send_rows.reshape(experts, CAP, model_width), group_start, group_size, 1
    )
    group_grads = lax.dynamic_slice_in_dim(
        send_grads.reshape(experts, CAP, model_width), group_start, group_size, 1
    )
    fan_rows = jnp.repeat(group_rows, shards, axis=0)
    fan_grads = jnp.repeat(group_grads, shards, axis=0)
    gate_full, up_full = (
        lax.all_gather(gate_weight, "rep", axis=0, tiled=True),
        lax.all_gather(up_weight, "rep", axis=0, tiled=True),
    )
    down_full = lax.all_gather(down_weight, "rep", axis=1, tiled=True)
    hid_here = gate_full.shape[1]
    recv_rows = lax.all_to_all(fan_rows, "exp", split_axis=0, concat_axis=0, tiled=True)
    flat = recv_rows.reshape(-1, model_width)
    pre_gate = jnp.dot(flat, gate_full, preferred_element_type=jnp.float32)
    pre_up = jnp.dot(flat, up_full, preferred_element_type=jnp.float32)
    forward_hidden = (jax.nn.silu(pre_gate) * pre_up).astype(jnp.bfloat16)
    part = jnp.dot(forward_hidden, down_full, preferred_element_type=jnp.float32).astype(
        jnp.bfloat16
    )
    part, hidden, pre_gate, pre_up = (
        part.reshape(recv_rows.shape),
        forward_hidden,
        pre_gate,
        pre_up,
    )
    returned = lax.all_to_all(part, "exp", split_axis=0, concat_axis=0, tiled=True)
    recv_grads = lax.all_to_all(fan_grads, "exp", split_axis=0, concat_axis=0, tiled=True)
    flat = recv_grads.reshape(-1, model_width)
    grad_hidden = lax.dot_general(
        flat, down_full, (((1,), (1,)), ((), ())), preferred_element_type=jnp.float32
    )
    sigma = jax.nn.sigmoid(pre_gate)
    backward_grad_gate_pre = (
        grad_hidden * pre_up * sigma * (1.0 + pre_gate * (1.0 - sigma))
    ).astype(jnp.bfloat16)
    backward_grad_up_pre = (grad_hidden * pre_gate * sigma).astype(jnp.bfloat16)
    back = lax.dot_general(
        backward_grad_gate_pre,
        gate_full,
        (((1,), (1,)), ((), ())),
        preferred_element_type=jnp.float32,
    )
    back = back + lax.dot_general(
        backward_grad_up_pre, up_full, (((1,), (1,)), ((), ())), preferred_element_type=jnp.float32
    )
    back, grad_gate_pre, grad_up_pre = (
        back.astype(jnp.bfloat16).reshape(recv_grads.shape),
        backward_grad_gate_pre,
        backward_grad_up_pre,
    )
    returned_back = lax.all_to_all(back, "exp", split_axis=0, concat_axis=0, tiled=True)
    group_out = jnp.sum(
        returned.reshape(experts, shards, group_size, model_width).astype(jnp.float32), axis=1
    ).astype(jnp.bfloat16)
    group_back = jnp.sum(
        returned_back.reshape(experts, shards, group_size, model_width).astype(jnp.float32), axis=1
    ).astype(jnp.bfloat16)
    slot_out, slot_back = (
        lax.all_gather(group_out, "rep", axis=1, tiled=True),
        lax.all_gather(group_back, "rep", axis=1, tiled=True),
    )
    slot_out = slot_out.reshape(slots, model_width).astype(jnp.float32)
    slot_back = slot_back.reshape(slots, model_width).astype(jnp.float32)
    expert_out = slot_out[slot_index].reshape(tok_here, top_count, model_width)
    expert_back = slot_back[slot_index].reshape(tok_here, top_count, model_width)
    mixed = (stem_value + jnp.sum(gates[:, :, None] * expert_out, axis=1)).astype(jnp.bfloat16)
    grad_gates = jnp.sum(upstream[:, None, :] * expert_out, axis=-1)
    _, gate_pull = jax.vjp(gating, picked)
    grad_picked = gate_pull(grad_gates)[0]
    selector = (routes[:, :, None] == jnp.arange(experts, dtype=jnp.int32)).astype(jnp.float32)
    grad_logits = jnp.sum(selector * grad_picked[:, :, None], axis=1)
    grad_normed = jnp.sum(expert_back, axis=1) + jnp.dot(
        grad_logits, router_weight.astype(jnp.float32).T, precision=lax.Precision.HIGHEST
    )
    _, norm_pull = jax.vjp(lambda values: rms_norm(values, norm_gain), stem_value)
    grad_stem = (upstream + norm_pull(grad_normed)[0]).astype(jnp.bfloat16)
    grad_block = with_halo(grad_stem.reshape(rows_here, width, model_width), (("exp", 0),), 1)
    projected = jnp.dot(
        grad_block.reshape(-1, model_width), stem_weight.T, preferred_element_type=jnp.float32
    )
    projected = projected.reshape(rows_here + 2, width, 9, channels)
    shifted = jnp.pad(projected, ((0, 0), (1, 1), (0, 0), (0, 0)))
    terms = [
        shifted[2 - i : 2 - i + rows_here, 2 - j : 2 - j + width, 3 * i + j, :]
        for i in range(3)
        for j in range(3)
    ]
    grad_latent = jnp.sum(jnp.stack(terms, axis=0), axis=0).transpose(0, 2, 1)
    flat_rows = recv_rows.reshape(-1, model_width)
    flat_grads = recv_grads.reshape(-1, model_width)
    dims = (((0,), (0,)), ((), ()))
    term_gate = lax.dot_general(flat_rows, grad_gate_pre, dims, preferred_element_type=jnp.float32)
    term_up = lax.dot_general(flat_rows, grad_up_pre, dims, preferred_element_type=jnp.float32)
    term_down = lax.dot_general(flat_grads, hidden, dims, preferred_element_type=jnp.float32)
    summed = lax.psum_scatter(
        jnp.concatenate([term_gate, term_up, term_down], axis=1).astype(jnp.bfloat16),
        "rep",
        scatter_dimension=0,
        tiled=True,
    ).astype(jnp.float32)
    grad_gate = summed[:, :hid_here]
    grad_up = summed[:, hid_here : 2 * hid_here]
    grad_down = summed[:, 2 * hid_here :].T
    return (mixed, grad_latent, grad_gate, grad_up, grad_down)


def solution(mesh):
    return jax.shard_map(
        local,
        mesh=mesh,
        in_specs=(
            P("exp", None, None),
            P(),
            P(),
            P(),
            P("exp", None),
            P("rep", "exp"),
            P("rep", "exp"),
            P("exp", "rep"),
            P("exp", None),
        ),
        out_specs=(
            P("exp", None),
            P("exp", None, None),
            P("rep", "exp"),
            P("rep", "exp"),
            P("exp", "rep"),
        ),
        check_vma=False,
    )
```

profile of v0, /device:TPU:6, one launch (start us, length us, event | category | flops | bytes accessed | tf_op | source)
XLA Modules:
  0.0 458.4 jit_solution(8518326553651853229)
XLA Ops:
  7.9 11.7 %collective-permute-start.1 = (bf16[1,16,64]{2,1,0:T(8,128)(2,1)S(1)}, bf16[1,16,64]{2,1,0:T(8,128)(2,1)S(1)}, u32[]{:S(2)}, u32[]{:S(2)}) collective-permute-start(bf16[1,16,64]{2,1,0:T(8,128)(2,1)S(1)} %get-tuple-element.55), channel_id=1, source_target_pairs={{8,0},{16,8},{24,16},{32,24},{40,32},{48,40},{56,48},{64,56},{72,6... | collective-permute-start | bytes 6152 | tf_op jit(solution)/shard_map/ppermute | solution.py:19
  35.5 3.0 reshape.269
  38.5 3.4 scatter_custom_fusion
  41.9 2.9 scatter_custom_fusion.1
  47.3 11.0 %all-to-all-start = ((bf16[64,5,1536]{2,1,0:T(8,128)(2,1)}), bf16[64,5,1536]{2,1,0:T(8,128)(2,1)S(1)}, u32[]{:S(2)}, u32[]{:S(2)}) async-start(bf16[64,5,1536]{2,1,0:T(8,128)(2,1)} %bitcast.108), calls=%async_computation | async-start | bytes 3145728 | tf_op jit(solution)/shard_map/all_to_all | solution.py:99
  59.1 74.8 %all-to-all-done = bf16[64,5,1536]{2,1,0:T(8,128)(2,1)S(1)} async-done(((bf16[64,5,1536]{2,1,0:T(8,128)(2,1)}), bf16[64,5,1536]{2,1,0:T(8,128)(2,1)S(1)}, u32[]{:S(2)}, u32[]{:S(2)}) %all-to-all-start) | async-done | bytes 983072 | tf_op jit(solution)/shard_map/all_to_all | solution.py:99
  135.7 7.1 %all-to-all-start.2 = ((bf16[64,5,1536]{2,1,0:T(8,128)(2,1)}), bf16[64,5,1536]{2,1,0:T(8,128)(2,1)}, u32[]{:S(2)}, u32[]{:S(2)}) async-start(bf16[64,5,1536]{2,1,0:T(8,128)(2,1)} %bitcast.107), calls=%async_computation.2 | async-start | bytes 3145728 | tf_op jit(solution)/shard_map/all_to_all | solution.py:114
  145.9 73.0 %all-to-all-done.2 = bf16[64,5,1536]{2,1,0:T(8,128)(2,1)} async-done(((bf16[64,5,1536]{2,1,0:T(8,128)(2,1)}), bf16[64,5,1536]{2,1,0:T(8,128)(2,1)}, u32[]{:S(2)}, u32[]{:S(2)}) %all-to-all-start.2) | async-done | bytes 983072 | tf_op jit(solution)/shard_map/all_to_all | solution.py:114
  226.7 3.4 multiply_convert_fusion.3
  233.7 7.3 %all-to-all-start.3 = ((bf16[64,5,1536]{2,1,0:T(8,128)(2,1)}), bf16[64,5,1536]{2,1,0:T(8,128)(2,1)}, u32[]{:S(2)}, u32[]{:S(2)}) async-start(bf16[64,5,1536]{2,1,0:T(8,128)(2,1)} %reshape.233), calls=%async_computation.3 | async-start | bytes 3145728 | tf_op jit(solution)/shard_map/all_to_all | solution.py:138
  250.2 66.9 %all-to-all-done.3 = bf16[64,5,1536]{2,1,0:T(8,128)(2,1)} async-done(((bf16[64,5,1536]{2,1,0:T(8,128)(2,1)}), bf16[64,5,1536]{2,1,0:T(8,128)(2,1)}, u32[]{:S(2)}, u32[]{:S(2)}) %all-to-all-start.3) | async-done | bytes 983072 | tf_op jit(solution)/shard_map/all_to_all | solution.py:138
  317.1 7.1 %all-to-all-start.1 = ((bf16[64,5,1536]{2,1,0:T(8,128)(2,1)}), bf16[64,5,1536]{2,1,0:T(8,128)(2,1)}, u32[]{:S(2)}, u32[]{:S(2)}) async-start(bf16[64,5,1536]{2,1,0:T(8,128)(2,1)} %reshape.227), calls=%async_computation.1 | async-start | bytes 3145728 | tf_op jit(solution)/shard_map/all_to_all | solution.py:113
  324.3 3.2 pad_maximum_fusion
  327.5 5.8 %copy.115 = bf16[1536,1152]{1,0:T(8,128)(2,1)} copy(bf16[1536,1152]{0,1:T(8,128)(2,1)} %pad_maximum_fusion) | data formatting | bytes 7077888
  337.1 14.1 %all_gather.19 = bf16[8,40,1536]{2,0,1:T(8,128)(2,1)S(1)} all-gather(bf16[8,5,1536]{2,0,1:T(8,128)(2,1)S(1)} %copy.107), channel_id=1, replica_groups=mesh['exp'=64,'rep'=8] {'rep'}, dimensions={1}, use_global_device_ids=true | all-gather | bytes 1105920 | tf_op jit(solution)/shard_map/all_gather | solution.py:147
  353.9 3.1 reshape.235
  356.9 43.4 %all-to-all-done.1 = bf16[64,5,1536]{2,1,0:T(8,128)(2,1)} async-done(((bf16[64,5,1536]{2,1,0:T(8,128)(2,1)}), bf16[64,5,1536]{2,1,0:T(8,128)(2,1)}, u32[]{:S(2)}, u32[]{:S(2)}) %all-to-all-start.1) | async-done | bytes 983072 | tf_op jit(solution)/shard_map/all_to_all | solution.py:113
  402.1 14.5 %all_gather.18 = bf16[8,40,1536]{2,0,1:T(8,128)(2,1)S(1)} all-gather(bf16[8,5,1536]{2,0,1:T(8,128)(2,1)S(1)} %copy.104), channel_id=1, replica_groups=mesh['exp'=64,'rep'=8] {'rep'}, dimensions={1}, use_global_device_ids=true | all-gather | bytes 1105920 | tf_op jit(solution)/shard_map/all_gather | solution.py:146
  419.3 3.1 reshape.229
  422.4 5.0 %multiply_reduce_fusion = (f32[128,2]{1,0:T(8,128)S(1)}, f32[128,1536]{1,0:T(8,128)}) fusion(f32[128,2,1536]{2,1,0:T(2,128)} %reshape.229, f32[128,1536]{1,0:T(8,128)} %convert_element_type.77, f32[128,2]{1,0:T(8,128)S(1)} %copy.100), kind=kLoop, calls=%fused_computation.18 | loop fusion | flops 1376000 | bytes 3147776 | tf_op jit(solution)/shard_map/reduce_sum | solution.py:154
  427.5 3.0 reduce_sum.177
  435.5 3.9 collective-permute-start.2
  439.4 3.2 collective-permute-done.3
  442.6 4.0 collective-permute-done.2
  (145 shorter events, 66.1 us)
Async XLA Ops:
  7.2 23.8 %copy-start = (bf16[144,1536]{1,0:T(8,128)(2,1)S(1)}, bf16[144,1536]{1,0:T(8,128)(2,1)}, u32[]{:S(2)}) copy-start(bf16[144,1536]{1,0:T(8,128)(2,1)} %param.10) | copy-start | bytes 1327108
  7.9 22.5 %collective-permute-start.1 = (bf16[1,16,64]{2,1,0:T(8,128)(2,1)S(1)}, bf16[1,16,64]{2,1,0:T(8,128)(2,1)S(1)}, u32[]{:S(2)}, u32[]{:S(2)}) collective-permute-start(bf16[1,16,64]{2,1,0:T(8,128)(2,1)S(1)} %get-tuple-element.55), channel_id=1, source_target_pairs={{8,0},{16,8},{24,16},{32,24},{40,32},{48,40},{56,48},{64,56},{72,6... | collective-permute-start | bytes 6152 | tf_op jit(solution)/shard_map/ppermute | solution.py:19
  19.6 10.8 %collective-permute-start = (bf16[1,16,64]{2,1,0:T(8,128)(2,1)S(1)}, bf16[1,16,64]{2,1,0:T(8,128)(2,1)S(1)}, u32[]{:S(2)}, u32[]{:S(2)}) collective-permute-start(bf16[1,16,64]{2,1,0:T(8,128)(2,1)S(1)} %get-tuple-element.54), channel_id=1, source_target_pairs={{0,8},{8,16},{16,24},{24,32},{32,40},{40,48},{48,56},{56,64},{64,7... | collective-permute-start | bytes 6152 | tf_op jit(solution)/shard_map/ppermute | solution.py:17
  27.7 2.7 copy-start.13
  30.1 1.9 copy-start.14
  47.3 86.6 %all-to-all-start = ((bf16[64,5,1536]{2,1,0:T(8,128)(2,1)}), bf16[64,5,1536]{2,1,0:T(8,128)(2,1)S(1)}, u32[]{:S(2)}, u32[]{:S(2)}) async-start(bf16[64,5,1536]{2,1,0:T(8,128)(2,1)} %bitcast.108), calls=%async_computation | async-start | bytes 3145728 | tf_op jit(solution)/shard_map/all_to_all | solution.py:99
  58.4 162.8 %all-gather.4.cloned.1.call-start = ((), (), s32[]{:S(2)}) async-start(), calls=%async_computation.5 | async-start | bytes 1327104 | tf_op jit(solution)/shard_map/all_gather | solution.py:94
  135.7 83.2 %all-to-all-start.2 = ((bf16[64,5,1536]{2,1,0:T(8,128)(2,1)}), bf16[64,5,1536]{2,1,0:T(8,128)(2,1)}, u32[]{:S(2)}, u32[]{:S(2)}) async-start(bf16[64,5,1536]{2,1,0:T(8,128)(2,1)} %bitcast.107), calls=%async_computation.2 | async-start | bytes 3145728 | tf_op jit(solution)/shard_map/all_to_all | solution.py:114
  142.8 81.2 %all-gather.6.cloned.1.call-start = ((), (), s32[]{:S(2)}) async-start(), calls=%async_computation.6 | async-start | bytes 1327104 | tf_op jit(solution)/shard_map/all_gather | solution.py:95
  143.5 83.1 %all-gather.8.cloned.1.call-start = ((), (), s32[]{:S(2)}) async-start(), calls=%async_computation.7 | async-start | bytes 1327104 | tf_op jit(solution)/shard_map/all_gather | solution.py:97
  226.7 3.4 copy-start.3
  233.7 7.3 %copy-start.12 = (bf16[320,384]{1,0:T(8,128)(2,1)S(1)}, bf16[320,384]{1,0:T(8,128)(2,1)}, u32[]{:S(2)}) copy-start(bf16[320,384]{1,0:T(8,128)(2,1)} %get-tuple-element.47) | copy-start | bytes 737284
  233.7 83.4 %all-to-all-start.3 = ((bf16[64,5,1536]{2,1,0:T(8,128)(2,1)}), bf16[64,5,1536]{2,1,0:T(8,128)(2,1)}, u32[]{:S(2)}, u32[]{:S(2)}) async-start(bf16[64,5,1536]{2,1,0:T(8,128)(2,1)} %reshape.233), calls=%async_computation.3 | async-start | bytes 3145728 | tf_op jit(solution)/shard_map/all_to_all | solution.py:138
  244.4 2.1 copy-start.11
  246.5 1.9 copy-start.9
  317.1 83.3 %all-to-all-start.1 = ((bf16[64,5,1536]{2,1,0:T(8,128)(2,1)}), bf16[64,5,1536]{2,1,0:T(8,128)(2,1)}, u32[]{:S(2)}, u32[]{:S(2)}) async-start(bf16[64,5,1536]{2,1,0:T(8,128)(2,1)} %reshape.227), calls=%async_computation.1 | async-start | bytes 3145728 | tf_op jit(solution)/shard_map/all_to_all | solution.py:113
  324.2 123.6 %reduce-scatter.4.cloned.1.call-start = ((), (), s32[]{:S(2)}) async-start(), calls=%async_computation.8 | async-start | bytes 3981312
  422.4 5.1 %copy-start.2 = (f32[128,2,1536]{2,1,0:T(2,128)S(1)}, f32[128,2,1536]{2,1,0:T(2,128)}, u32[]{:S(2)}) copy-start(f32[128,2,1536]{2,1,0:T(2,128)} %reshape.235) | copy-start | bytes 4718596
  430.5 1.9 copy-start.20
  430.5 1.9 copy-start.6
  430.5 2.0 copy-start.7
  430.5 2.0 copy-start.18
  433.5 9.0 %collective-permute-start.3 = (bf16[1,64,1536]{2,1,0:T(8,128)(2,1)S(1)}, bf16[1,64,1536]{2,1,0:T(8,128)(2,1)S(1)}, u32[]{:S(2)}, u32[]{:S(2)}) collective-permute-start(bf16[1,64,1536]{2,1,0:T(8,128)(2,1)S(1)} %get-tuple-element.53), channel_id=1, source_target_pairs={{8,0},{16,8},{24,16},{32,24},{40,32},{48,40},{56,48},{64,56},{72,6... | collective-permute-start | bytes 589832 | tf_op jit(solution)/shard_map/ppermute | solution.py:19
  435.5 11.1 %collective-permute-start.2 = (bf16[1,64,1536]{2,1,0:T(8,128)(2,1)S(1)}, bf16[1,64,1536]{2,1,0:T(8,128)(2,1)S(1)}, u32[]{:S(2)}, u32[]{:S(2)}) collective-permute-start(bf16[1,64,1536]{2,1,0:T(8,128)(2,1)S(1)} %get-tuple-element.52), channel_id=1, source_target_pairs={{0,8},{8,16},{16,24},{24,32},{32,40},{40,48},{48,56},{56,64},{64,7... | collective-permute-start | bytes 589832 | tf_op jit(solution)/shard_map/ppermute | solution.py:17
  (9 other events, 10.2 us)
Sparse Core Ops, SparseCore 0:
  61.3 31.8 all-gather.3
  145.7 31.8 all-gather.5
  179.8 31.0 all-gather.7
  333.4 45.9 reduce-scatter.3
where the time goes:
time: 460 us; the launch traced here: 458 us
  waiting for transfers between devices  267 us (58%)
  starting transfers between devices  52.3 us (11%)
  local copies, waits for them, and re-layouts  52.1 us (11%)
  blocking collectives  28.6 us (6%)
  other arithmetic  22.8 us (5%)
  matrix products  21 us (5%)
  between operations  14.3 us (3%)
    all_to_all x1, waiting for transfers between devices, local(): lax.all_to_all(fan_rows, 'exp', split_axis=0, concat_axis=0, tiled=True)  74.8 us
    all_to_all x1, waiting for transfers between devices, local(): lax.all_to_all(fan_grads, 'exp', split_axis=0, concat_axis=0, tiled=True)  73 us
    all_to_all x1, waiting for transfers between devices, local(): lax.all_to_all(back, 'exp', split_axis=0, concat_axis=0, tiled=True)  66.9 us
    all_to_all x1, waiting for transfers between devices, local(): lax.all_to_all(part, 'exp', split_axis=0, concat_axis=0, tiled=True)  43.4 us
    all_gather x1, blocking collectives, local(): lax.all_gather(group_out, 'rep', axis=1, tiled=True)  14.5 us
    all_gather x1, blocking collectives, local(): lax.all_gather(group_back, 'rep', axis=1, tiled=True)  14.1 us
    ppermute x2, starting transfers between devices, with_halo(): lax.ppermute(head, axis, [((i + 1) % count, i) for i in range(ends)])  13.6 us
    unnamed x54, local copies, waits for them, and re-layouts  13.1 us
  transfers between devices with their start and end apart: 12, of which 6 were waited for; matrix products, arithmetic and copies ran while one was open for 14% of the time, Pallas kernels for 0%

commit v1 on v0

--- a/solution.py
+++ b/solution.py
@@ -1,9 +1,20 @@
+import functools
 import jax
 import jax.numpy as jnp
 from jax import lax
 from jax.sharding import PartitionSpec as P
 
 CAP = 40
+
+
+def make_the_case(mat, out_dim):
+    piece_next = jnp.concatenate(
+        lax.all_to_all(jnp.stack([mat] * lax.axis_size("rep"), 0), "rep", 0, 0), out_dim
+    )
+    return piece_next
+
+
+save_the_roads = functools.partial(make_the_case, out_dim=1)
 
 
 def with_halo(cells, sides, width):
@@ -144,7 +155,7 @@
     ).astype(jnp.bfloat16)
     slot_out, slot_back = (
         lax.all_gather(group_out, "rep", axis=1, tiled=True),
-        lax.all_gather(group_back, "rep", axis=1, tiled=True),
+        save_the_roads(group_back),
     )
     slot_out = slot_out.reshape(slots, model_width).astype(jnp.float32)
     slot_back = slot_back.reshape(slots, model_width).astype(jnp.float32)

time: 460 us -> 483 us (1.050)
  waiting for transfers between devices: 267 us -> 289 us
  blocking collectives: 28.6 us -> 22.3 us
    all_to_all x1, waiting for transfers between devices: 43.4 us -> 61.9 us  [local(): lax.all_to_all(part, 'exp', split_axis=0, concat_axis=0, tiled=True)]
    all_gather x1 -> x0, blocking collectives: 14.1 us -> none  [local(): lax.all_gather(group_back, 'rep', axis=1, tiled=True)]
    all_gather x1, blocking collectives: 14.5 us -> 22.3 us  [local(): lax.all_gather(group_out, 'rep', axis=1, tiled=True)]
    unnamed x54 -> x50, local copies, waits for them, and re-layouts: 13.1 us -> 13.1 us
  transfers between devices with their start and end apart: 12 -> 13, of which waited for: 6 -> 6; matrix products, arithmetic and copies ran while one was open for 14% -> 14% of each run, Pallas kernels for 0% -> 0%
where the time goes in v1:
time: 483 us; the launch traced here: 481 us
  waiting for transfers between devices  289 us (60%)
  starting transfers between devices  56.8 us (12%)
  local copies, waits for them, and re-layouts  56 us (12%)
  other arithmetic  22.7 us (5%)
  blocking collectives  22.3 us (5%)
  matrix products  19.9 us (4%)
  between operations  14.3 us (3%)
    all_to_all x1, waiting for transfers between devices, local(): lax.all_to_all(fan_rows, 'exp', split_axis=0, concat_axis=0, tiled=True)  74.8 us
    all_to_all x1, waiting for transfers between devices, local(): lax.all_to_all(fan_grads, 'exp', split_axis=0, concat_axis=0, tiled=True)  73 us
    all_to_all x1, waiting for transfers between devices, local(): lax.all_to_all(back, 'exp', split_axis=0, concat_axis=0, tiled=True)  70.6 us
    all_to_all x1, waiting for transfers between devices, local(): lax.all_to_all(part, 'exp', split_axis=0, concat_axis=0, tiled=True)  61.9 us
    all_gather x1, blocking collectives, local(): lax.all_gather(group_out, 'rep', axis=1, tiled=True)  22.3 us
    ppermute x2, starting transfers between devices, with_halo(): lax.ppermute(head, axis, [((i + 1) % count, i) for i in range(ends)])  13.6 us
    unnamed x50, local copies, waits for them, and re-layouts  13.1 us
    all_to_all x1, starting transfers between devices, local(): lax.all_to_all(fan_rows, 'exp', split_axis=0, concat_axis=0, tiled=True)  11 us
  transfers between devices with their start and end apart: 13, of which 6 were waited for; matrix products, arithmetic and copies ran while one was open for 14% of the time, Pallas kernels for 0%

profile of v1, /device:TPU:6, one launch (start us, length us, event | category | flops | bytes accessed | tf_op | source)
XLA Modules:
  0.0 481.4 jit_solution(4304654060023835509)
XLA Ops:
  7.9 11.7 %collective-permute-start.1 = (bf16[1,16,64]{2,1,0:T(8,128)(2,1)S(1)}, bf16[1,16,64]{2,1,0:T(8,128)(2,1)S(1)}, u32[]{:S(2)}, u32[]{:S(2)}) collective-permute-start(bf16[1,16,64]{2,1,0:T(8,128)(2,1)S(1)} %get-tuple-element.55), channel_id=1, source_target_pairs={{8,0},{16,8},{24,16},{32,24},{40,32},{48,40},{56,48},{64,56},{72,6... | collective-permute-start | bytes 6152 | tf_op jit(solution)/shard_map/ppermute | solution.py:30
  35.5 3.0 reshape.271
  38.5 3.4 scatter_custom_fusion
  41.9 2.9 scatter_custom_fusion.1
  47.3 11.0 %all-to-all-start = ((bf16[64,5,1536]{2,1,0:T(8,128)(2,1)}), bf16[64,5,1536]{2,1,0:T(8,128)(2,1)S(1)}, u32[]{:S(2)}, u32[]{:S(2)}) async-start(bf16[64,5,1536]{2,1,0:T(8,128)(2,1)} %bitcast.108), calls=%async_computation | async-start | bytes 3145728 | tf_op jit(solution)/shard_map/all_to_all | solution.py:110
  59.1 74.8 %all-to-all-done = bf16[64,5,1536]{2,1,0:T(8,128)(2,1)S(1)} async-done(((bf16[64,5,1536]{2,1,0:T(8,128)(2,1)}), bf16[64,5,1536]{2,1,0:T(8,128)(2,1)S(1)}, u32[]{:S(2)}, u32[]{:S(2)}) %all-to-all-start) | async-done | bytes 983072 | tf_op jit(solution)/shard_map/all_to_all | solution.py:110
  135.7 7.1 %all-to-all-start.2 = ((bf16[64,5,1536]{2,1,0:T(8,128)(2,1)}), bf16[64,5,1536]{2,1,0:T(8,128)(2,1)}, u32[]{:S(2)}, u32[]{:S(2)}) async-start(bf16[64,5,1536]{2,1,0:T(8,128)(2,1)} %bitcast.107), calls=%async_computation.2 | async-start | bytes 3145728 | tf_op jit(solution)/shard_map/all_to_all | solution.py:125
  145.9 73.0 %all-to-all-done.2 = bf16[64,5,1536]{2,1,0:T(8,128)(2,1)} async-done(((bf16[64,5,1536]{2,1,0:T(8,128)(2,1)}), bf16[64,5,1536]{2,1,0:T(8,128)(2,1)}, u32[]{:S(2)}, u32[]{:S(2)}) %all-to-all-start.2) | async-done | bytes 983072 | tf_op jit(solution)/shard_map/all_to_all | solution.py:125
  221.2 2.7 fusion.42
  223.9 2.7 fusion.43
  226.7 3.4 multiply_convert_fusion.3
  233.6 7.3 %all-to-all-start.3 = ((bf16[64,5,1536]{2,1,0:T(8,128)(2,1)}), bf16[64,5,1536]{2,1,0:T(8,128)(2,1)}, u32[]{:S(2)}, u32[]{:S(2)}) async-start(bf16[64,5,1536]{2,1,0:T(8,128)(2,1)} %reshape.235), calls=%async_computation.3 | async-start | bytes 3145728 | tf_op jit(solution)/shard_map/all_to_all | solution.py:149
  246.4 70.6 %all-to-all-done.3 = bf16[64,5,1536]{2,1,0:T(8,128)(2,1)} async-done(((bf16[64,5,1536]{2,1,0:T(8,128)(2,1)}), bf16[64,5,1536]{2,1,0:T(8,128)(2,1)}, u32[]{:S(2)}, u32[]{:S(2)}) %all-to-all-start.3) | async-done | bytes 983072 | tf_op jit(solution)/shard_map/all_to_all | solution.py:149
  317.0 7.1 %all-to-all-start.1 = ((bf16[64,5,1536]{2,1,0:T(8,128)(2,1)}), bf16[64,5,1536]{2,1,0:T(8,128)(2,1)}, u32[]{:S(2)}, u32[]{:S(2)}) async-start(bf16[64,5,1536]{2,1,0:T(8,128)(2,1)} %reshape.229), calls=%async_computation.1 | async-start | bytes 3145728 | tf_op jit(solution)/shard_map/all_to_all | solution.py:124
  328.8 5.8 %copy.115 = bf16[1536,1152]{1,0:T(8,128)(2,1)} copy(bf16[1536,1152]{0,1:T(8,128)(2,1)} %pad_maximum_fusion) | data formatting | bytes 7077888
  338.4 61.9 %all-to-all-done.1 = bf16[64,5,1536]{2,1,0:T(8,128)(2,1)} async-done(((bf16[64,5,1536]{2,1,0:T(8,128)(2,1)}), bf16[64,5,1536]{2,1,0:T(8,128)(2,1)}, u32[]{:S(2)}, u32[]{:S(2)}) %all-to-all-start.1) | async-done | bytes 983072 | tf_op jit(solution)/shard_map/all_to_all | solution.py:124
  401.3 4.5 all-to-all-start.4
  407.6 22.3 %all_gather.15 = bf16[8,40,1536]{2,0,1:T(8,128)(2,1)S(1)} all-gather(bf16[8,5,1536]{2,0,1:T(8,128)(2,1)S(1)} %copy.104), channel_id=1, replica_groups=mesh['exp'=64,'rep'=8] {'rep'}, dimensions={1}, use_global_device_ids=true | all-gather | bytes 1105920 | tf_op jit(solution)/shard_map/all_gather | solution.py:157
  434.8 4.6 multiply_reduce_fusion
  441.0 2.9 copy.108
  450.5 3.0 reduce_sum.177
  458.4 3.9 collective-permute-start.2
  462.4 3.2 collective-permute-done.3
  465.6 4.0 collective-permute-done.2
  (145 shorter events, 70.2 us)
Async XLA Ops:
  7.2 23.8 %copy-start = (bf16[144,1536]{1,0:T(8,128)(2,1)S(1)}, bf16[144,1536]{1,0:T(8,128)(2,1)}, u32[]{:S(2)}) copy-start(bf16[144,1536]{1,0:T(8,128)(2,1)} %param.10) | copy-start | bytes 1327108
  7.9 22.5 %collective-permute-start.1 = (bf16[1,16,64]{2,1,0:T(8,128)(2,1)S(1)}, bf16[1,16,64]{2,1,0:T(8,128)(2,1)S(1)}, u32[]{:S(2)}, u32[]{:S(2)}) collective-permute-start(bf16[1,16,64]{2,1,0:T(8,128)(2,1)S(1)} %get-tuple-element.55), channel_id=1, source_target_pairs={{8,0},{16,8},{24,16},{32,24},{40,32},{48,40},{56,48},{64,56},{72,6... | collective-permute-start | bytes 6152 | tf_op jit(solution)/shard_map/ppermute | solution.py:30
  19.6 10.8 %collective-permute-start = (bf16[1,16,64]{2,1,0:T(8,128)(2,1)S(1)}, bf16[1,16,64]{2,1,0:T(8,128)(2,1)S(1)}, u32[]{:S(2)}, u32[]{:S(2)}) collective-permute-start(bf16[1,16,64]{2,1,0:T(8,128)(2,1)S(1)} %get-tuple-element.54), channel_id=1, source_target_pairs={{0,8},{8,16},{16,24},{24,32},{32,40},{40,48},{48,56},{56,64},{64,7... | collective-permute-start | bytes 6152 | tf_op jit(solution)/shard_map/ppermute | solution.py:28
  27.7 2.7 copy-start.11
  30.1 1.8 copy-start.13
  30.1 1.9 copy-start.12
  47.3 86.6 %all-to-all-start = ((bf16[64,5,1536]{2,1,0:T(8,128)(2,1)}), bf16[64,5,1536]{2,1,0:T(8,128)(2,1)S(1)}, u32[]{:S(2)}, u32[]{:S(2)}) async-start(bf16[64,5,1536]{2,1,0:T(8,128)(2,1)} %bitcast.108), calls=%async_computation | async-start | bytes 3145728 | tf_op jit(solution)/shard_map/all_to_all | solution.py:110
  58.4 162.8 %all-gather.4.cloned.1.call-start = ((), (), s32[]{:S(2)}) async-start(), calls=%async_computation.6 | async-start | bytes 1327104 | tf_op jit(solution)/shard_map/all_gather | solution.py:105
  135.7 83.2 %all-to-all-start.2 = ((bf16[64,5,1536]{2,1,0:T(8,128)(2,1)}), bf16[64,5,1536]{2,1,0:T(8,128)(2,1)}, u32[]{:S(2)}, u32[]{:S(2)}) async-start(bf16[64,5,1536]{2,1,0:T(8,128)(2,1)} %bitcast.107), calls=%async_computation.2 | async-start | bytes 3145728 | tf_op jit(solution)/shard_map/all_to_all | solution.py:125
  142.8 81.2 %all-gather.6.cloned.1.call-start = ((), (), s32[]{:S(2)}) async-start(), calls=%async_computation.7 | async-start | bytes 1327104 | tf_op jit(solution)/shard_map/all_gather | solution.py:106
  143.5 83.1 %all-gather.8.cloned.1.call-start = ((), (), s32[]{:S(2)}) async-start(), calls=%async_computation.8 | async-start | bytes 1327104 | tf_op jit(solution)/shard_map/all_gather | solution.py:108
  226.7 3.4 copy-start.2
  233.6 7.3 %copy-start.10 = (bf16[320,384]{1,0:T(8,128)(2,1)S(1)}, bf16[320,384]{1,0:T(8,128)(2,1)}, u32[]{:S(2)}) copy-start(bf16[320,384]{1,0:T(8,128)(2,1)} %get-tuple-element.47) | copy-start | bytes 737284
  233.6 83.4 %all-to-all-start.3 = ((bf16[64,5,1536]{2,1,0:T(8,128)(2,1)}), bf16[64,5,1536]{2,1,0:T(8,128)(2,1)}, u32[]{:S(2)}, u32[]{:S(2)}) async-start(bf16[64,5,1536]{2,1,0:T(8,128)(2,1)} %reshape.235), calls=%async_computation.3 | async-start | bytes 3145728 | tf_op jit(solution)/shard_map/all_to_all | solution.py:149
  317.0 83.3 %all-to-all-start.1 = ((bf16[64,5,1536]{2,1,0:T(8,128)(2,1)}), bf16[64,5,1536]{2,1,0:T(8,128)(2,1)}, u32[]{:S(2)}, u32[]{:S(2)}) async-start(bf16[64,5,1536]{2,1,0:T(8,128)(2,1)} %reshape.229), calls=%async_computation.1 | async-start | bytes 3145728 | tf_op jit(solution)/shard_map/all_to_all | solution.py:124
  324.2 146.7 %reduce-scatter.4.cloned.1.call-start = ((), (), s32[]{:S(2)}) async-start(), calls=%async_computation.9 | async-start | bytes 3981312
  324.2 1.8 copy-start.8
  401.3 38.2 %all-to-all-start.4 = ((bf16[8,8,5,1536]{3,1,2,0:T(8,128)(2,1)}), bf16[8,8,5,1536]{3,1,2,0:T(8,128)(2,1)}, u32[]{:S(2)}, u32[]{:S(2)}) async-start(bf16[8,8,5,1536]{3,1,2,0:T(8,128)(2,1)} %stack.52), calls=%async_computation.4 | async-start | bytes 1966080 | tf_op jit(solution)/shard_map/all_to_all | solution.py:12
  453.5 1.9 copy-start.18
  453.5 1.9 copy-start.5
  453.5 1.9 copy-start.6
  453.5 1.9 copy-start.16
  456.5 9.1 %collective-permute-start.3 = (bf16[1,64,1536]{2,1,0:T(8,128)(2,1)S(1)}, bf16[1,64,1536]{2,1,0:T(8,128)(2,1)S(1)}, u32[]{:S(2)}, u32[]{:S(2)}) collective-permute-start(bf16[1,64,1536]{2,1,0:T(8,128)(2,1)S(1)} %get-tuple-element.53), channel_id=1, source_target_pairs={{8,0},{16,8},{24,16},{32,24},{40,32},{48,40},{56,48},{64,56},{72,6... | collective-permute-start | bytes 589832 | tf_op jit(solution)/shard_map/ppermute | solution.py:30
  458.4 11.2 %collective-permute-start.2 = (bf16[1,64,1536]{2,1,0:T(8,128)(2,1)S(1)}, bf16[1,64,1536]{2,1,0:T(8,128)(2,1)S(1)}, u32[]{:S(2)}, u32[]{:S(2)}) collective-permute-start(bf16[1,64,1536]{2,1,0:T(8,128)(2,1)S(1)} %get-tuple-element.52), channel_id=1, source_target_pairs={{0,8},{8,16},{16,24},{24,32},{32,40},{40,48},{48,56},{56,64},{64,7... | collective-permute-start | bytes 589832 | tf_op jit(solution)/shard_map/ppermute | solution.py:28
  (8 other events, 8.4 us)
Sparse Core Ops, SparseCore 0:
  61.3 31.8 all-gather.3
  145.7 31.8 all-gather.5
  179.8 31.0 all-gather.7
  334.8 45.9 reduce-scatter.3
